TPU v7x, 128 devices: a whole 4x4x4 slice. The times are simulated.
128 devices in a mesh: blk: 16 (over x_lo, y, core), head: 8 (over x_hi, z).
Axes of the slice: x: 4 (x_hi: 2, x_lo: 2; x = x_hi * 2 + x_lo), y: 4, z: 4, core: 2. Of those that a mesh axis runs over, the one named last changes fastest.
Arguments:
- queries: bfloat16 [16384, 3072], P(('blk', 'head')), may hold values from -100 to 100
- keys: bfloat16 [16384, 3072], P(('blk', 'head')), may hold values from -100 to 100
- values: bfloat16 [16384, 3072], P(('blk', 'head')), may hold values from -6 to 6
- query_gain: float32 [3072], replicated, may hold values from 1 to 4
- key_gain: float32 [3072], replicated, may hold values from 0.1 to 1.9
Outputs:
- attended: bfloat16 [16384, 3072], P(('blk', 'head'))
All inputs are finite; a program needn't handle non-finite values.
Results may differ from a plain program's by a relative error of at most 0.0075.
The roundings to bfloat16 on the way count: a program that leaves them out, or rounds other values in their place, can miss the bound.
Values may be sent and summed in bfloat16 or wider, within the bound.
A program may use at most 128 MiB of HBM per device.

v0:
```python
import math
import jax
import jax.numpy as jnp
from jax import lax
from jax.sharding import PartitionSpec as P

HEAD_DIM = 128


def normalize(block, gain):
    wide = block.astype(jnp.float32)
    mean_sq = jnp.mean(wide * wide, axis=-1, keepdims=True)
    return (wide * lax.rsqrt(mean_sq + 1e-06) * gain).astype(jnp.bfloat16)


def absorb(carry, pieces, q_heads, factor):
    run_max, run_sum, accum = carry
    key_block, value_block = pieces
    scores = (
        jnp.einsum("qhd,khd->hqk", q_heads, key_block, preferred_element_type=jnp.float32) * factor
    )
    new_max = jnp.maximum(run_max, jnp.max(scores, axis=-1))
    shrink = jnp.exp(run_max - new_max)
    weights = jnp.exp(scores - new_max[:, :, None])
    new_sum = run_sum * shrink + jnp.sum(weights, axis=-1)
    mixed = jnp.einsum(
        "hqk,khd->hqd",
        weights.astype(jnp.bfloat16),
        value_block,
        preferred_element_type=jnp.float32,
    )
    return (new_max, new_sum, accum * shrink[:, :, None] + mixed)


def shards(queries, keys, values, query_gain, key_gain):
    group = lax.axis_size("head")
    width = queries.shape[1] // group
    heads_here = width // HEAD_DIM
    factor = 1.0 / math.sqrt(HEAD_DIM)
    first_part = normalize(queries, query_gain)
    second_part = normalize(keys, key_gain)
    q_local, k_local, v_local = (
        lax.all_to_all(first_part, "head", split_axis=1, concat_axis=0, tiled=True),
        lax.all_to_all(second_part, "head", split_axis=1, concat_axis=0, tiled=True),
        lax.all_to_all(values, "head", split_axis=1, concat_axis=0, tiled=True),
    )
    rows = q_local.shape[0]
    q_heads = q_local.reshape(rows, heads_here, HEAD_DIM)
    k_heads = k_local.reshape(rows, heads_here, HEAD_DIM)
    v_heads = v_local.reshape(rows, heads_here, HEAD_DIM)
    start_state = (
        jnp.full((heads_here, rows), -jnp.inf, jnp.float32),
        jnp.zeros((heads_here, rows), jnp.float32),
        jnp.zeros((heads_here, rows, HEAD_DIM), jnp.float32),
    )
    key_piece = lax.all_gather(k_heads, "blk", axis=0, tiled=True)
    value_piece = lax.all_gather(v_heads, "blk", axis=0, tiled=True)
    length = key_piece.shape[0]
    block_rows = math.gcd(length, 1024)
    count = length // block_rows
    key_blocks = key_piece.reshape(count, block_rows, heads_here, HEAD_DIM)
    value_blocks = value_piece.reshape(count, block_rows, heads_here, HEAD_DIM)

    def step_fn(state, blocks):
        return (absorb(state, blocks, q_heads, factor), None)

    final_state, unused = lax.scan(step_fn, start_state, (key_blocks, value_blocks))
    run_max, run_sum, accum = final_state
    result = accum / run_sum[:, :, None]
    result = jnp.transpose(result, (1, 0, 2)).reshape(rows, width).astype(jnp.bfloat16)
    return lax.all_to_all(result, "head", split_axis=0, concat_axis=1, tiled=True)


def solution(mesh):
    placed = (
        P(("blk", "head"), None),
        P(("blk", "head"), None),
        P(("blk", "head"), None),
        P(),
        P(),
    )
    return jax.shard_map(
        shards, mesh=mesh, in_specs=placed, out_specs=P(("blk", "head"), None), check_vma=False
    )
```

profile of v0, /device:TPU:0, one launch (start us, length us, event | category | flops | bytes accessed | tf_op | source)
XLA Modules:
  0.0 578.3 jit_solution(14939098089677855722)
XLA Ops:
  9.7 22.0 %all_to_all.64 = bf16[128,8,384]{0,2,1:T(8,128)(2,1)S(1)} all-to-all(bf16[128,8,384]{0,2,1:T(8,128)(2,1)S(1)} %bitcast.64), channel_id=1, replica_groups=mesh['blk'=16,'head'=8] {'head'}, dimensions={1} | all-to-all | bytes 1572864 | tf_op jit(solution)/shard_map/all_to_all | solution.py:44
  33.9 21.0 %all_to_all.65 = bf16[128,8,384]{0,2,1:T(8,128)(2,1)S(1)} all-to-all(bf16[128,8,384]{0,2,1:T(8,128)(2,1)S(1)} %bitcast.70), channel_id=1, replica_groups=mesh['blk'=16,'head'=8] {'head'}, dimensions={1} | all-to-all | bytes 1572864 | tf_op jit(solution)/shard_map/all_to_all | solution.py:45
  62.2 18.7 %all-to-all-done.1 = bf16[128,8,384]{0,2,1:T(8,128)(2,1)S(1)} async-done(((bf16[128,8,384]{0,2,1:T(8,128)(2,1)}), bf16[128,8,384]{0,2,1:T(8,128)(2,1)S(1)}, u32[]{:S(2)}, u32[]{:S(2)}) %all-to-all-start.1) | async-done | bytes 786464 | tf_op jit(solution)/shard_map/all_to_all | solution.py:43
  82.8 31.2 %all-gather.3.cloned.1.call-done = bf16[16384,3,128]{0,2,1:T(8,128)(2,1)} async-done(((bf16[1024,3,128]{0,2,1:T(8,128)(2,1)}), bf16[16384,3,128]{0,2,1:T(8,128)(2,1)}) %all-gather.3.cloned.1.call-update) | async-done | bytes 12582928 | tf_op jit(solution)/shard_map/all_gather | solution.py:56
  114.0 16.7 %copy.32 = bf16[16384,3,128]{2,0,1:T(8,128)(2,1)} copy(bf16[16384,3,128]{0,2,1:T(8,128)(2,1)} %all-gather.3.cloned.1.call-done) | data formatting | bytes 25165824 | tf_op jit(solution)/shard_map/all_gather | solution.py:56
  130.7 59.0 %all-gather.5.cloned.1.call-done = bf16[16384,3,128]{0,2,1:T(8,128)(2,1)} async-done(((bf16[1024,3,128]{0,2,1:T(8,128)(2,1)}), bf16[16384,3,128]{0,2,1:T(8,128)(2,1)}) %all-gather.5.cloned.1.call-update) | async-done | bytes 12582928 | tf_op jit(solution)/shard_map/all_gather | solution.py:57
  189.6 16.6 %copy.37 = bf16[16384,3,128]{2,0,1:T(8,128)(2,1)} copy(bf16[16384,3,128]{0,2,1:T(8,128)(2,1)} %all-gather.5.cloned.1.call-done) | data formatting | bytes 25165824 | tf_op jit(solution)/shard_map/all_gather | solution.py:57
  206.2 340.2 %while.15 = (s32[]{:T(128)}, f32[3,1024]{1,0:T(4,128)S(1)}, f32[3,1024]{1,0:T(4,128)S(1)}, f32[3,1024,128]{2,1,0:T(8,128)}, bf16[16,1024,3,128]{3,1,0,2:T(8,128)...) while((s32[]{:T(128)}, f32[3,1024]{1,0:T(4,128)S(1)}, ...), condition=%wide.region_5.6_spmd.clone, body=%wide.region_2.5_spmd.clone.sunk | while | flops 1636973568 | bytes 93783168 | solution.py:67
  206.2 7.8 %bitcast_reduce_fusion.2 = (f32[3,1024]{1,0:T(4,128)S(1)}, f32[3,1024,1024]{2,1,0:T(8,128)}) fusion(bf16[1024,3,128]{2,0,1:T(8,128)(2,1)} %get-tuple-element.182, bf16[16,1024,3,128]{3,1,0,2:T(8,128)(2,1)} %get-tuple-element.181, s32[]{:T(128)} %get-tuple-element.168), kind=kOutput, calls=%fused_computation.1.clone.1 | convolution fusion | flops 811594752 | bytes 14168576 | tf_op jit(solution)/shard_map/while/body/eval_jaxpr/qhd,khd->hqk/dot_general | solution.py:20
  214.0 6.8 %fusion.36 = f32[3,1024]{1,0:T(4,128)S(1)} fusion(f32[3,1024,1024]{2,1,0:T(8,128)} %get-tuple-element.156, f32[3,1024]{1,0:T(4,128)S(1)} %select_maximum_fusion.2), kind=kLoop, calls=%fused_computation.4.clone.1 | loop fusion | flops 9434112 | bytes 12607488 | tf_op jit(solution)/shard_map/while/body/eval_jaxpr/reduce_sum | solution.py:25
  227.3 7.8 %bitcast_reduce_fusion.2 = (f32[3,1024]{1,0:T(4,128)S(1)}, f32[3,1024,1024]{2,1,0:T(8,128)}) fusion(bf16[1024,3,128]{2,0,1:T(8,128)(2,1)} %get-tuple-element.182, bf16[16,1024,3,128]{3,1,0,2:T(8,128)(2,1)} %get-tuple-element.181, s32[]{:T(128)} %get-tuple-element.168), kind=kOutput, calls=%fused_computation.1.clone.1 | convolution fusion | flops 811594752 | bytes 14168576 | tf_op jit(solution)/shard_map/while/body/eval_jaxpr/qhd,khd->hqk/dot_general | solution.py:20
  235.0 6.8 %fusion.36 = f32[3,1024]{1,0:T(4,128)S(1)} fusion(f32[3,1024,1024]{2,1,0:T(8,128)} %get-tuple-element.156, f32[3,1024]{1,0:T(4,128)S(1)} %select_maximum_fusion.2), kind=kLoop, calls=%fused_computation.4.clone.1 | loop fusion | flops 9434112 | bytes 12607488 | tf_op jit(solution)/shard_map/while/body/eval_jaxpr/reduce_sum | solution.py:25
  248.5 7.8 %bitcast_reduce_fusion.2 = (f32[3,1024]{1,0:T(4,128)S(1)}, f32[3,1024,1024]{2,1,0:T(8,128)}) fusion(bf16[1024,3,128]{2,0,1:T(8,128)(2,1)} %get-tuple-element.182, bf16[16,1024,3,128]{3,1,0,2:T(8,128)(2,1)} %get-tuple-element.181, s32[]{:T(128)} %get-tuple-element.168), kind=kOutput, calls=%fused_computation.1.clone.1 | convolution fusion | flops 811594752 | bytes 14168576 | tf_op jit(solution)/shard_map/while/body/eval_jaxpr/qhd,khd->hqk/dot_general | solution.py:20
  256.3 6.8 %fusion.36 = f32[3,1024]{1,0:T(4,128)S(1)} fusion(f32[3,1024,1024]{2,1,0:T(8,128)} %get-tuple-element.156, f32[3,1024]{1,0:T(4,128)S(1)} %select_maximum_fusion.2), kind=kLoop, calls=%fused_computation.4.clone.1 | loop fusion | flops 9434112 | bytes 12607488 | tf_op jit(solution)/shard_map/while/body/eval_jaxpr/reduce_sum | solution.py:25
  269.8 7.8 %bitcast_reduce_fusion.2 = (f32[3,1024]{1,0:T(4,128)S(1)}, f32[3,1024,1024]{2,1,0:T(8,128)}) fusion(bf16[1024,3,128]{2,0,1:T(8,128)(2,1)} %get-tuple-element.182, bf16[16,1024,3,128]{3,1,0,2:T(8,128)(2,1)} %get-tuple-element.181, s32[]{:T(128)} %get-tuple-element.168), kind=kOutput, calls=%fused_computation.1.clone.1 | convolution fusion | flops 811594752 | bytes 14168576 | tf_op jit(solution)/shard_map/while/body/eval_jaxpr/qhd,khd->hqk/dot_general | solution.py:20
  277.6 6.8 %fusion.36 = f32[3,1024]{1,0:T(4,128)S(1)} fusion(f32[3,1024,1024]{2,1,0:T(8,128)} %get-tuple-element.156, f32[3,1024]{1,0:T(4,128)S(1)} %select_maximum_fusion.2), kind=kLoop, calls=%fused_computation.4.clone.1 | loop fusion | flops 9434112 | bytes 12607488 | tf_op jit(solution)/shard_map/while/body/eval_jaxpr/reduce_sum | solution.py:25
  291.1 7.8 %bitcast_reduce_fusion.2 = (f32[3,1024]{1,0:T(4,128)S(1)}, f32[3,1024,1024]{2,1,0:T(8,128)}) fusion(bf16[1024,3,128]{2,0,1:T(8,128)(2,1)} %get-tuple-element.182, bf16[16,1024,3,128]{3,1,0,2:T(8,128)(2,1)} %get-tuple-element.181, s32[]{:T(128)} %get-tuple-element.168), kind=kOutput, calls=%fused_computation.1.clone.1 | convolution fusion | flops 811594752 | bytes 14168576 | tf_op jit(solution)/shard_map/while/body/eval_jaxpr/qhd,khd->hqk/dot_general | solution.py:20
  298.9 6.8 %fusion.36 = f32[3,1024]{1,0:T(4,128)S(1)} fusion(f32[3,1024,1024]{2,1,0:T(8,128)} %get-tuple-element.156, f32[3,1024]{1,0:T(4,128)S(1)} %select_maximum_fusion.2), kind=kLoop, calls=%fused_computation.4.clone.1 | loop fusion | flops 9434112 | bytes 12607488 | tf_op jit(solution)/shard_map/while/body/eval_jaxpr/reduce_sum | solution.py:25
  312.4 7.8 %bitcast_reduce_fusion.2 = (f32[3,1024]{1,0:T(4,128)S(1)}, f32[3,1024,1024]{2,1,0:T(8,128)}) fusion(bf16[1024,3,128]{2,0,1:T(8,128)(2,1)} %get-tuple-element.182, bf16[16,1024,3,128]{3,1,0,2:T(8,128)(2,1)} %get-tuple-element.181, s32[]{:T(128)} %get-tuple-element.168), kind=kOutput, calls=%fused_computation.1.clone.1 | convolution fusion | flops 811594752 | bytes 14168576 | tf_op jit(solution)/shard_map/while/body/eval_jaxpr/qhd,khd->hqk/dot_general | solution.py:20
  320.1 6.8 %fusion.36 = f32[3,1024]{1,0:T(4,128)S(1)} fusion(f32[3,1024,1024]{2,1,0:T(8,128)} %get-tuple-element.156, f32[3,1024]{1,0:T(4,128)S(1)} %select_maximum_fusion.2), kind=kLoop, calls=%fused_computation.4.clone.1 | loop fusion | flops 9434112 | bytes 12607488 | tf_op jit(solution)/shard_map/while/body/eval_jaxpr/reduce_sum | solution.py:25
  333.7 7.8 %bitcast_reduce_fusion.2 = (f32[3,1024]{1,0:T(4,128)S(1)}, f32[3,1024,1024]{2,1,0:T(8,128)}) fusion(bf16[1024,3,128]{2,0,1:T(8,128)(2,1)} %get-tuple-element.182, bf16[16,1024,3,128]{3,1,0,2:T(8,128)(2,1)} %get-tuple-element.181, s32[]{:T(128)} %get-tuple-element.168), kind=kOutput, calls=%fused_computation.1.clone.1 | convolution fusion | flops 811594752 | bytes 14168576 | tf_op jit(solution)/shard_map/while/body/eval_jaxpr/qhd,khd->hqk/dot_general | solution.py:20
  341.4 6.8 %fusion.36 = f32[3,1024]{1,0:T(4,128)S(1)} fusion(f32[3,1024,1024]{2,1,0:T(8,128)} %get-tuple-element.156, f32[3,1024]{1,0:T(4,128)S(1)} %select_maximum_fusion.2), kind=kLoop, calls=%fused_computation.4.clone.1 | loop fusion | flops 9434112 | bytes 12607488 | tf_op jit(solution)/shard_map/while/body/eval_jaxpr/reduce_sum | solution.py:25
  354.9 7.8 %bitcast_reduce_fusion.2 = (f32[3,1024]{1,0:T(4,128)S(1)}, f32[3,1024,1024]{2,1,0:T(8,128)}) fusion(bf16[1024,3,128]{2,0,1:T(8,128)(2,1)} %get-tuple-element.182, bf16[16,1024,3,128]{3,1,0,2:T(8,128)(2,1)} %get-tuple-element.181, s32[]{:T(128)} %get-tuple-element.168), kind=kOutput, calls=%fused_computation.1.clone.1 | convolution fusion | flops 811594752 | bytes 14168576 | tf_op jit(solution)/shard_map/while/body/eval_jaxpr/qhd,khd->hqk/dot_general | solution.py:20
  376.2 7.8 %bitcast_reduce_fusion.2 = (f32[3,1024]{1,0:T(4,128)S(1)}, f32[3,1024,1024]{2,1,0:T(8,128)}) fusion(bf16[1024,3,128]{2,0,1:T(8,128)(2,1)} %get-tuple-element.182, bf16[16,1024,3,128]{3,1,0,2:T(8,128)(2,1)} %get-tuple-element.181, s32[]{:T(128)} %get-tuple-element.168), kind=kOutput, calls=%fused_computation.1.clone.1 | convolution fusion | flops 811594752 | bytes 14168576 | tf_op jit(solution)/shard_map/while/body/eval_jaxpr/qhd,khd->hqk/dot_general | solution.py:20
  397.5 7.8 %bitcast_reduce_fusion.2 = (f32[3,1024]{1,0:T(4,128)S(1)}, f32[3,1024,1024]{2,1,0:T(8,128)}) fusion(bf16[1024,3,128]{2,0,1:T(8,128)(2,1)} %get-tuple-element.182, bf16[16,1024,3,128]{3,1,0,2:T(8,128)(2,1)} %get-tuple-element.181, s32[]{:T(128)} %get-tuple-element.168), kind=kOutput, calls=%fused_computation.1.clone.1 | convolution fusion | flops 811594752 | bytes 14168576 | tf_op jit(solution)/shard_map/while/body/eval_jaxpr/qhd,khd->hqk/dot_general | solution.py:20
  418.8 7.8 %bitcast_reduce_fusion.2 = (f32[3,1024]{1,0:T(4,128)S(1)}, f32[3,1024,1024]{2,1,0:T(8,128)}) fusion(bf16[1024,3,128]{2,0,1:T(8,128)(2,1)} %get-tuple-element.182, bf16[16,1024,3,128]{3,1,0,2:T(8,128)(2,1)} %get-tuple-element.181, s32[]{:T(128)} %get-tuple-element.168), kind=kOutput, calls=%fused_computation.1.clone.1 | convolution fusion | flops 811594752 | bytes 14168576 | tf_op jit(solution)/shard_map/while/body/eval_jaxpr/qhd,khd->hqk/dot_general | solution.py:20
  440.1 7.8 %bitcast_reduce_fusion.2 = (f32[3,1024]{1,0:T(4,128)S(1)}, f32[3,1024,1024]{2,1,0:T(8,128)}) fusion(bf16[1024,3,128]{2,0,1:T(8,128)(2,1)} %get-tuple-element.182, bf16[16,1024,3,128]{3,1,0,2:T(8,128)(2,1)} %get-tuple-element.181, s32[]{:T(128)} %get-tuple-element.168), kind=kOutput, calls=%fused_computation.1.clone.1 | convolution fusion | flops 811594752 | bytes 14168576 | tf_op jit(solution)/shard_map/while/body/eval_jaxpr/qhd,khd->hqk/dot_general | solution.py:20
  461.3 7.8 %bitcast_reduce_fusion.2 = (f32[3,1024]{1,0:T(4,128)S(1)}, f32[3,1024,1024]{2,1,0:T(8,128)}) fusion(bf16[1024,3,128]{2,0,1:T(8,128)(2,1)} %get-tuple-element.182, bf16[16,1024,3,128]{3,1,0,2:T(8,128)(2,1)} %get-tuple-element.181, s32[]{:T(128)} %get-tuple-element.168), kind=kOutput, calls=%fused_computation.1.clone.1 | convolution fusion | flops 811594752 | bytes 14168576 | tf_op jit(solution)/shard_map/while/body/eval_jaxpr/qhd,khd->hqk/dot_general | solution.py:20
  482.6 7.8 %bitcast_reduce_fusion.2 = (f32[3,1024]{1,0:T(4,128)S(1)}, f32[3,1024,1024]{2,1,0:T(8,128)}) fusion(bf16[1024,3,128]{2,0,1:T(8,128)(2,1)} %get-tuple-element.182, bf16[16,1024,3,128]{3,1,0,2:T(8,128)(2,1)} %get-tuple-element.181, s32[]{:T(128)} %get-tuple-element.168), kind=kOutput, calls=%fused_computation.1.clone.1 | convolution fusion | flops 811594752 | bytes 14168576 | tf_op jit(solution)/shard_map/while/body/eval_jaxpr/qhd,khd->hqk/dot_general | solution.py:20
  503.9 7.8 %bitcast_reduce_fusion.2 = (f32[3,1024]{1,0:T(4,128)S(1)}, f32[3,1024,1024]{2,1,0:T(8,128)}) fusion(bf16[1024,3,128]{2,0,1:T(8,128)(2,1)} %get-tuple-element.182, bf16[16,1024,3,128]{3,1,0,2:T(8,128)(2,1)} %get-tuple-element.181, s32[]{:T(128)} %get-tuple-element.168), kind=kOutput, calls=%fused_computation.1.clone.1 | convolution fusion | flops 811594752 | bytes 14168576 | tf_op jit(solution)/shard_map/while/body/eval_jaxpr/qhd,khd->hqk/dot_general | solution.py:20
  525.2 7.8 %bitcast_reduce_fusion.2 = (f32[3,1024]{1,0:T(4,128)S(1)}, f32[3,1024,1024]{2,1,0:T(8,128)}) fusion(bf16[1024,3,128]{2,0,1:T(8,128)(2,1)} %get-tuple-element.182, bf16[16,1024,3,128]{3,1,0,2:T(8,128)(2,1)} %get-tuple-element.181, s32[]{:T(128)} %get-tuple-element.168), kind=kOutput, calls=%fused_computation.1.clone.1 | convolution fusion | flops 811594752 | bytes 14168576 | tf_op jit(solution)/shard_map/while/body/eval_jaxpr/qhd,khd->hqk/dot_general | solution.py:20
  548.9 21.4 %all_to_all.66 = bf16[8,128,384]{1,2,0:T(8,128)(2,1)S(1)} all-to-all(bf16[8,128,384]{1,2,0:T(8,128)(2,1)S(1)} %copy.42), channel_id=1, replica_groups=mesh['blk'=16,'head'=8] {'head'}, dimensions={0} | all-to-all | bytes 1572864 | tf_op jit(solution)/shard_map/all_to_all | solution.py:71
  (140 shorter events, 186.5 us)
Async XLA Ops:
  6.5 107.5 %all-gather.3.cloned.1.call-start = ((), (), s32[]{:S(2)}) async-start(), calls=%async_computation.4 | async-start | bytes 13369344 | tf_op jit(solution)/shard_map/all_gather | solution.py:56
  32.2 1.3 copy-start.2
  33.5 156.2 %all-gather.5.cloned.1.call-start = ((), (), s32[]{:S(2)}) async-start(), calls=%async_computation.5 | async-start | bytes 13369344 | tf_op jit(solution)/shard_map/all_gather | solution.py:57
  55.4 1.3 copy-start.1
  55.4 1.5 copy-start.3
  58.4 22.4 %all-to-all-start.1 = ((bf16[128,8,384]{0,2,1:T(8,128)(2,1)}), bf16[128,8,384]{0,2,1:T(8,128)(2,1)S(1)}, u32[]{:S(2)}, u32[]{:S(2)}) async-start(bf16[128,8,384]{0,2,1:T(8,128)(2,1)} %bitcast.3), calls=%async_computation.1 | async-start | bytes 1572864 | tf_op jit(solution)/shard_map/all_to_all | solution.py:43
  214.0 8.2 %copy-start = (f32[3,1024,1024]{2,1,0:T(8,128)S(1)}, f32[3,1024,1024]{2,1,0:T(8,128)}, u32[]{:S(2)}) copy-start(f32[3,1024,1024]{2,1,0:T(8,128)} %get-tuple-element.156) | copy-start | bytes 37748740 | tf_op jit(solution)/shard_map/while
  235.0 8.2 %copy-start = (f32[3,1024,1024]{2,1,0:T(8,128)S(1)}, f32[3,1024,1024]{2,1,0:T(8,128)}, u32[]{:S(2)}) copy-start(f32[3,1024,1024]{2,1,0:T(8,128)} %get-tuple-element.156) | copy-start | bytes 37748740 | tf_op jit(solution)/shard_map/while
  256.3 8.2 %copy-start = (f32[3,1024,1024]{2,1,0:T(8,128)S(1)}, f32[3,1024,1024]{2,1,0:T(8,128)}, u32[]{:S(2)}) copy-start(f32[3,1024,1024]{2,1,0:T(8,128)} %get-tuple-element.156) | copy-start | bytes 37748740 | tf_op jit(solution)/shard_map/while
  277.6 8.2 %copy-start = (f32[3,1024,1024]{2,1,0:T(8,128)S(1)}, f32[3,1024,1024]{2,1,0:T(8,128)}, u32[]{:S(2)}) copy-start(f32[3,1024,1024]{2,1,0:T(8,128)} %get-tuple-element.156) | copy-start | bytes 37748740 | tf_op jit(solution)/shard_map/while
  298.9 8.2 %copy-start = (f32[3,1024,1024]{2,1,0:T(8,128)S(1)}, f32[3,1024,1024]{2,1,0:T(8,128)}, u32[]{:S(2)}) copy-start(f32[3,1024,1024]{2,1,0:T(8,128)} %get-tuple-element.156) | copy-start | bytes 37748740 | tf_op jit(solution)/shard_map/while
  320.1 8.2 %copy-start = (f32[3,1024,1024]{2,1,0:T(8,128)S(1)}, f32[3,1024,1024]{2,1,0:T(8,128)}, u32[]{:S(2)}) copy-start(f32[3,1024,1024]{2,1,0:T(8,128)} %get-tuple-element.156) | copy-start | bytes 37748740 | tf_op jit(solution)/shard_map/while
  341.4 8.2 %copy-start = (f32[3,1024,1024]{2,1,0:T(8,128)S(1)}, f32[3,1024,1024]{2,1,0:T(8,128)}, u32[]{:S(2)}) copy-start(f32[3,1024,1024]{2,1,0:T(8,128)} %get-tuple-element.156) | copy-start | bytes 37748740 | tf_op jit(solution)/shard_map/while
  362.7 8.2 %copy-start = (f32[3,1024,1024]{2,1,0:T(8,128)S(1)}, f32[3,1024,1024]{2,1,0:T(8,128)}, u32[]{:S(2)}) copy-start(f32[3,1024,1024]{2,1,0:T(8,128)} %get-tuple-element.156) | copy-start | bytes 37748740 | tf_op jit(solution)/shard_map/while
  384.0 8.2 %copy-start = (f32[3,1024,1024]{2,1,0:T(8,128)S(1)}, f32[3,1024,1024]{2,1,0:T(8,128)}, u32[]{:S(2)}) copy-start(f32[3,1024,1024]{2,1,0:T(8,128)} %get-tuple-element.156) | copy-start | bytes 37748740 | tf_op jit(solution)/shard_map/while
  405.3 8.2 %copy-start = (f32[3,1024,1024]{2,1,0:T(8,128)S(1)}, f32[3,1024,1024]{2,1,0:T(8,128)}, u32[]{:S(2)}) copy-start(f32[3,1024,1024]{2,1,0:T(8,128)} %get-tuple-element.156) | copy-start | bytes 37748740 | tf_op jit(solution)/shard_map/while
  426.5 8.2 %copy-start = (f32[3,1024,1024]{2,1,0:T(8,128)S(1)}, f32[3,1024,1024]{2,1,0:T(8,128)}, u32[]{:S(2)}) copy-start(f32[3,1024,1024]{2,1,0:T(8,128)} %get-tuple-element.156) | copy-start | bytes 37748740 | tf_op jit(solution)/shard_map/while
  447.8 8.2 %copy-start = (f32[3,1024,1024]{2,1,0:T(8,128)S(1)}, f32[3,1024,1024]{2,1,0:T(8,128)}, u32[]{:S(2)}) copy-start(f32[3,1024,1024]{2,1,0:T(8,128)} %get-tuple-element.156) | copy-start | bytes 37748740 | tf_op jit(solution)/shard_map/while
  469.1 8.2 %copy-start = (f32[3,1024,1024]{2,1,0:T(8,128)S(1)}, f32[3,1024,1024]{2,1,0:T(8,128)}, u32[]{:S(2)}) copy-start(f32[3,1024,1024]{2,1,0:T(8,128)} %get-tuple-element.156) | copy-start | bytes 37748740 | tf_op jit(solution)/shard_map/while
  490.4 8.2 %copy-start = (f32[3,1024,1024]{2,1,0:T(8,128)S(1)}, f32[3,1024,1024]{2,1,0:T(8,128)}, u32[]{:S(2)}) copy-start(f32[3,1024,1024]{2,1,0:T(8,128)} %get-tuple-element.156) | copy-start | bytes 37748740 | tf_op jit(solution)/shard_map/while
  511.7 8.2 %copy-start = (f32[3,1024,1024]{2,1,0:T(8,128)S(1)}, f32[3,1024,1024]{2,1,0:T(8,128)}, u32[]{:S(2)}) copy-start(f32[3,1024,1024]{2,1,0:T(8,128)} %get-tuple-element.156) | copy-start | bytes 37748740 | tf_op jit(solution)/shard_map/while
  532.9 8.2 %copy-start = (f32[3,1024,1024]{2,1,0:T(8,128)S(1)}, f32[3,1024,1024]{2,1,0:T(8,128)}, u32[]{:S(2)}) copy-start(f32[3,1024,1024]{2,1,0:T(8,128)} %get-tuple-element.156) | copy-start | bytes 37748740 | tf_op jit(solution)/shard_map/while
Sparse Core Ops, SparseCore 0:
  33.6 80.3 all-gather.2
  115.7 73.9 all-gather.4
where the time goes:
time: 580 us; the launch traced here: 578 us
  matrix products  209 us (36%)
  other arithmetic  114 us (20%)
  waiting for transfers between devices  109 us (19%)
  blocking collectives  64.4 us (11%)
  local copies, waits for them, and re-layouts  63.7 us (11%)
  between operations  13.6 us (2%)
    dot_general x16, matrix products, absorb(): jnp.einsum('qhd,khd->hqk', q_heads, key_block, preferred_element_type=jnp...  124 us
    reduce_sum x16, other arithmetic, absorb(): new_sum = run_sum * shrink + jnp.sum(weights, axis=-1)  109 us
    dot_general x16, matrix products, absorb(): jnp.einsum('hqk,khd->hqd', weights.astype(jnp.bfloat16), value_block, pre...  85.5 us
    all_gather x1, waiting for transfers between devices, shards(): value_piece = lax.all_gather(v_heads, 'blk', axis=0, tiled=True)  59 us
    all_gather x1, waiting for transfers between devices, shards(): key_piece = lax.all_gather(k_heads, 'blk', axis=0, tiled=True)  31.2 us
    all_to_all x1, blocking collectives, shards(): lax.all_to_all(second_part, 'head', split_axis=1, concat_axis=0, tiled=True)  22 us
    all_to_all x1, blocking collectives, shards(): lax.all_to_all(result, 'head', split_axis=0, concat_axis=1, tiled=True)  21.4 us
    while x48, local copies, waits for them, and re-layouts  21.4 us
  transfers between devices with their start and end apart: 3, of which 3 were waited for; matrix products, arithmetic and copies ran while one was open for 4% of the time, Pallas kernels for 0%

commit v1 on v0

--- a/solution.py
+++ b/solution.py
@@ -53,8 +53,11 @@
         jnp.zeros((heads_here, rows), jnp.float32),
         jnp.zeros((heads_here, rows, HEAD_DIM), jnp.float32),
     )
-    key_piece = lax.all_gather(k_heads, "blk", axis=0, tiled=True)
-    value_piece = lax.all_gather(v_heads, "blk", axis=0, tiled=True)
+    key_piece, value_piece = jnp.split(
+        lax.all_gather(jnp.concatenate([k_heads, v_heads], axis=1), "blk", axis=0, tiled=True),
+        [k_heads.shape[1]],
+        axis=1,
+    )
     length = key_piece.shape[0]
     block_rows = math.gcd(length, 1024)
     count = length // block_rows

time: 580 us -> 613 us (1.057)
  waiting for transfers between devices: 109 us -> 152 us
  blocking collectives: 64.4 us -> 22.1 us
  local copies, waits for them, and re-layouts: 63.7 us -> 81.7 us
  starting transfers between devices: 3.77 us -> 15.4 us
    split x0 -> x3, local copies, waits for them, and re-layouts: none -> 50.3 us  [shards(): jnp.split(lax.all_gather(jnp.concatenate([k_heads, v_heads], axis=1), 'bl...]
    all_to_all x2 -> x0, blocking collectives: 43 us -> none  [the longest x1 22 us: shards(): lax.all_to_all(second_part, 'head', split_axis=1, concat_axis=0, tiled=True)]
    all_gather x2 -> x0, local copies, waits for them, and re-layouts: 33.2 us -> none  [the longest x1 16.7 us: shards(): key_piece = lax.all_gather(k_heads, 'blk', axis=0, tiled=True)]
    all_to_all x0 -> x2, waiting for transfers between devices: none -> 24.9 us  [the longest x1 12.7 us: shards(): lax.all_to_all(values, 'head', split_axis=1, concat_axis=0, tiled=True)]
    all_gather x2 -> x1, waiting for transfers between devices: 90.1 us -> 107 us  [shards(): lax.all_gather(jnp.concatenate([k_heads, v_heads], axis=1), 'blk', axis=0...]
    all_to_all x0 -> x2, starting transfers between devices: none -> 11.6 us  [the longest x1 7.86 us: shards(): lax.all_to_all(second_part, 'head', split_axis=1, concat_axis=0, tiled=True)]
  transfers between devices with their start and end apart: 3 -> 4, of which waited for: 3 -> 4; matrix products, arithmetic and copies ran while one was open for 4% -> 1% of each run, Pallas kernels for 0% -> 0%
where the time goes in v1:
time: 613 us; the launch traced here: 611 us
  matrix products  210 us (34%)
  waiting for transfers between devices  152 us (25%)
  other arithmetic  116 us (19%)
  local copies, waits for them, and re-layouts  81.7 us (13%)
  blocking collectives  22.1 us (4%)
  starting transfers between devices  15.4 us (3%)
  between operations  13.5 us (2%)
    dot_general x16, matrix products, absorb(): jnp.einsum('qhd,khd->hqk', q_heads, key_block, preferred_element_type=jnp...  124 us
    reduce_sum x16, other arithmetic, absorb(): new_sum = run_sum * shrink + jnp.sum(weights, axis=-1)  109 us
    all_gather x1, waiting for transfers between devices, shards(): lax.all_gather(jnp.concatenate([k_heads, v_heads], axis=1), 'blk', axis=0...  107 us
    dot_general x16, matrix products, absorb(): jnp.einsum('hqk,khd->hqd', weights.astype(jnp.bfloat16), value_block, pre...  85.8 us
    split x3, local copies, waits for them, and re-layouts, shards(): jnp.split(lax.all_gather(jnp.concatenate([k_heads, v_heads], axis=1), 'bl...  50.3 us
    all_to_all x1, blocking collectives, shards(): lax.all_to_all(result, 'head', split_axis=0, concat_axis=1, tiled=True)  22.1 us
    while x48, local copies, waits for them, and re-layouts  21.4 us
    all_to_all x1, waiting for transfers between devices, shards(): lax.all_to_all(first_part, 'head', split_axis=1, concat_axis=0, tiled=True)  21 us
  transfers between devices with their start and end apart: 4, of which 4 were waited for; matrix products, arithmetic and copies ran while one was open for 1% of the time, Pallas kernels for 0%

profile of v1, /device:TPU:0, one launch (start us, length us, event | category | flops | bytes accessed | tf_op | source)
XLA Modules:
  0.0 611.0 jit_solution(6170507373256593090)
XLA Ops:
  10.5 7.9 %all-to-all-start = ((bf16[128,8,384]{0,2,1:T(8,128)(2,1)}), bf16[128,8,384]{0,2,1:T(8,128)(2,1)S(1)}, u32[]{:S(2)}, u32[]{:S(2)}) async-start(bf16[128,8,384]{0,2,1:T(8,128)(2,1)} %bitcast), calls=%async_computation | async-start | bytes 1572864 | tf_op jit(solution)/shard_map/all_to_all | solution.py:44
  19.5 12.2 %all-to-all-done = bf16[128,8,384]{0,2,1:T(8,128)(2,1)S(1)} async-done(((bf16[128,8,384]{0,2,1:T(8,128)(2,1)}), bf16[128,8,384]{0,2,1:T(8,128)(2,1)S(1)}, u32[]{:S(2)}, u32[]{:S(2)}) %all-to-all-start) | async-done | bytes 786464 | tf_op jit(solution)/shard_map/all_to_all | solution.py:44
  36.4 12.7 %all-to-all-done.1 = bf16[128,8,384]{0,2,1:T(8,128)(2,1)S(1)} async-done(((bf16[128,8,384]{0,2,1:T(8,128)(2,1)}), bf16[128,8,384]{0,2,1:T(8,128)(2,1)S(1)}, u32[]{:S(2)}, u32[]{:S(2)}) %all-to-all-start.1) | async-done | bytes 786464 | tf_op jit(solution)/shard_map/all_to_all | solution.py:45
  57.9 21.0 %all-to-all-done.2 = bf16[128,8,384]{0,2,1:T(8,128)(2,1)S(1)} async-done(((bf16[128,8,384]{0,2,1:T(8,128)(2,1)}), bf16[128,8,384]{0,2,1:T(8,128)(2,1)S(1)}, u32[]{:S(2)}, u32[]{:S(2)}) %all-to-all-start.2) | async-done | bytes 786464 | tf_op jit(solution)/shard_map/all_to_all | solution.py:43
  80.9 106.6 %all-gather.2.cloned.1.call-done = bf16[16384,6,128]{0,2,1:T(8,128)(2,1)} async-done(((bf16[1024,6,128]{0,2,1:T(8,128)(2,1)}), bf16[16384,6,128]{0,2,1:T(8,128)(2,1)}) %all-gather.2.cloned.1.call-update) | async-done | bytes 25165840 | tf_op jit(solution)/shard_map/all_gather | solution.py:57
  187.4 17.2 %fusion.26 = (bf16[16384,3,128]{0,2,1:T(8,128)(2,1)}, bf16[16384,3,128]{0,2,1:T(8,128)(2,1)}) fusion(bf16[16384,6,128]{0,2,1:T(8,128)(2,1)} %all-gather.2.cloned.1.call-done), kind=kLoop, calls=%fused_computation.37 | loop fusion | bytes 50331648 | tf_op jit(solution)/shard_map/split | solution.py:56
  204.6 16.5 %copy.34 = bf16[16384,3,128]{2,0,1:T(8,128)(2,1)} copy(bf16[16384,3,128]{0,2,1:T(8,128)(2,1)} %get-tuple-element.109) | data formatting | bytes 25165824 | tf_op jit(solution)/shard_map/split | solution.py:56
  221.1 16.6 %copy.37 = bf16[16384,3,128]{2,0,1:T(8,128)(2,1)} copy(bf16[16384,3,128]{0,2,1:T(8,128)(2,1)} %get-tuple-element.108) | data formatting | bytes 25165824 | tf_op jit(solution)/shard_map/split | solution.py:56
  237.7 340.8 %while.15 = (s32[]{:T(128)}, f32[3,1024]{1,0:T(4,128)S(1)}, f32[3,1024]{1,0:T(4,128)S(1)}, f32[3,1024,128]{2,1,0:T(8,128)}, bf16[16,1024,3,128]{3,1,0,2:T(8,128)...) while((s32[]{:T(128)}, f32[3,1024]{1,0:T(4,128)S(1)}, ...), condition=%wide.region_5.6_spmd.clone, body=%wide.region_2.5_spmd.clone.sunk | while | flops 1636973568 | bytes 93783168 | solution.py:70
  237.7 7.8 %bitcast_reduce_fusion.2 = (f32[3,1024]{1,0:T(4,128)S(1)}, f32[3,1024,1024]{2,1,0:T(8,128)}) fusion(bf16[1024,3,128]{2,0,1:T(8,128)(2,1)} %get-tuple-element.184, bf16[16,1024,3,128]{3,1,0,2:T(8,128)(2,1)} %get-tuple-element.183, s32[]{:T(128)} %get-tuple-element.170), kind=kOutput, calls=%fused_computation.1.clone.1 | convolution fusion | flops 811594752 | bytes 14168576 | tf_op jit(solution)/shard_map/while/body/eval_jaxpr/qhd,khd->hqk/dot_general | solution.py:20
  245.5 6.8 %fusion.37 = f32[3,1024]{1,0:T(4,128)S(1)} fusion(f32[3,1024,1024]{2,1,0:T(8,128)} %get-tuple-element.158, f32[3,1024]{1,0:T(4,128)S(1)} %select_maximum_fusion.2), kind=kLoop, calls=%fused_computation.4.clone.1 | loop fusion | flops 9434112 | bytes 12607488 | tf_op jit(solution)/shard_map/while/body/eval_jaxpr/reduce_sum | solution.py:25
  258.8 7.8 %bitcast_reduce_fusion.2 = (f32[3,1024]{1,0:T(4,128)S(1)}, f32[3,1024,1024]{2,1,0:T(8,128)}) fusion(bf16[1024,3,128]{2,0,1:T(8,128)(2,1)} %get-tuple-element.184, bf16[16,1024,3,128]{3,1,0,2:T(8,128)(2,1)} %get-tuple-element.183, s32[]{:T(128)} %get-tuple-element.170), kind=kOutput, calls=%fused_computation.1.clone.1 | convolution fusion | flops 811594752 | bytes 14168576 | tf_op jit(solution)/shard_map/while/body/eval_jaxpr/qhd,khd->hqk/dot_general | solution.py:20
  266.5 6.8 %fusion.37 = f32[3,1024]{1,0:T(4,128)S(1)} fusion(f32[3,1024,1024]{2,1,0:T(8,128)} %get-tuple-element.158, f32[3,1024]{1,0:T(4,128)S(1)} %select_maximum_fusion.2), kind=kLoop, calls=%fused_computation.4.clone.1 | loop fusion | flops 9434112 | bytes 12607488 | tf_op jit(solution)/shard_map/while/body/eval_jaxpr/reduce_sum | solution.py:25
  280.1 7.8 %bitcast_reduce_fusion.2 = (f32[3,1024]{1,0:T(4,128)S(1)}, f32[3,1024,1024]{2,1,0:T(8,128)}) fusion(bf16[1024,3,128]{2,0,1:T(8,128)(2,1)} %get-tuple-element.184, bf16[16,1024,3,128]{3,1,0,2:T(8,128)(2,1)} %get-tuple-element.183, s32[]{:T(128)} %get-tuple-element.170), kind=kOutput, calls=%fused_computation.1.clone.1 | convolution fusion | flops 811594752 | bytes 14168576 | tf_op jit(solution)/shard_map/while/body/eval_jaxpr/qhd,khd->hqk/dot_general | solution.py:20
  287.9 6.8 %fusion.37 = f32[3,1024]{1,0:T(4,128)S(1)} fusion(f32[3,1024,1024]{2,1,0:T(8,128)} %get-tuple-element.158, f32[3,1024]{1,0:T(4,128)S(1)} %select_maximum_fusion.2), kind=kLoop, calls=%fused_computation.4.clone.1 | loop fusion | flops 9434112 | bytes 12607488 | tf_op jit(solution)/shard_map/while/body/eval_jaxpr/reduce_sum | solution.py:25
  301.4 7.8 %bitcast_reduce_fusion.2 = (f32[3,1024]{1,0:T(4,128)S(1)}, f32[3,1024,1024]{2,1,0:T(8,128)}) fusion(bf16[1024,3,128]{2,0,1:T(8,128)(2,1)} %get-tuple-element.184, bf16[16,1024,3,128]{3,1,0,2:T(8,128)(2,1)} %get-tuple-element.183, s32[]{:T(128)} %get-tuple-element.170), kind=kOutput, calls=%fused_computation.1.clone.1 | convolution fusion | flops 811594752 | bytes 14168576 | tf_op jit(solution)/shard_map/while/body/eval_jaxpr/qhd,khd->hqk/dot_general | solution.py:20
  309.2 6.8 %fusion.37 = f32[3,1024]{1,0:T(4,128)S(1)} fusion(f32[3,1024,1024]{2,1,0:T(8,128)} %get-tuple-element.158, f32[3,1024]{1,0:T(4,128)S(1)} %select_maximum_fusion.2), kind=kLoop, calls=%fused_computation.4.clone.1 | loop fusion | flops 9434112 | bytes 12607488 | tf_op jit(solution)/shard_map/while/body/eval_jaxpr/reduce_sum | solution.py:25
  322.7 7.8 %bitcast_reduce_fusion.2 = (f32[3,1024]{1,0:T(4,128)S(1)}, f32[3,1024,1024]{2,1,0:T(8,128)}) fusion(bf16[1024,3,128]{2,0,1:T(8,128)(2,1)} %get-tuple-element.184, bf16[16,1024,3,128]{3,1,0,2:T(8,128)(2,1)} %get-tuple-element.183, s32[]{:T(128)} %get-tuple-element.170), kind=kOutput, calls=%fused_computation.1.clone.1 | convolution fusion | flops 811594752 | bytes 14168576 | tf_op jit(solution)/shard_map/while/body/eval_jaxpr/qhd,khd->hqk/dot_general | solution.py:20
  344.0 7.8 %bitcast_reduce_fusion.2 = (f32[3,1024]{1,0:T(4,128)S(1)}, f32[3,1024,1024]{2,1,0:T(8,128)}) fusion(bf16[1024,3,128]{2,0,1:T(8,128)(2,1)} %get-tuple-element.184, bf16[16,1024,3,128]{3,1,0,2:T(8,128)(2,1)} %get-tuple-element.183, s32[]{:T(128)} %get-tuple-element.170), kind=kOutput, calls=%fused_computation.1.clone.1 | convolution fusion | flops 811594752 | bytes 14168576 | tf_op jit(solution)/shard_map/while/body/eval_jaxpr/qhd,khd->hqk/dot_general | solution.py:20
  351.8 6.8 %fusion.37 = f32[3,1024]{1,0:T(4,128)S(1)} fusion(f32[3,1024,1024]{2,1,0:T(8,128)} %get-tuple-element.158, f32[3,1024]{1,0:T(4,128)S(1)} %select_maximum_fusion.2), kind=kLoop, calls=%fused_computation.4.clone.1 | loop fusion | flops 9434112 | bytes 12607488 | tf_op jit(solution)/shard_map/while/body/eval_jaxpr/reduce_sum | solution.py:25
  365.3 7.8 %bitcast_reduce_fusion.2 = (f32[3,1024]{1,0:T(4,128)S(1)}, f32[3,1024,1024]{2,1,0:T(8,128)}) fusion(bf16[1024,3,128]{2,0,1:T(8,128)(2,1)} %get-tuple-element.184, bf16[16,1024,3,128]{3,1,0,2:T(8,128)(2,1)} %get-tuple-element.183, s32[]{:T(128)} %get-tuple-element.170), kind=kOutput, calls=%fused_computation.1.clone.1 | convolution fusion | flops 811594752 | bytes 14168576 | tf_op jit(solution)/shard_map/while/body/eval_jaxpr/qhd,khd->hqk/dot_general | solution.py:20
  386.6 7.8 %bitcast_reduce_fusion.2 = (f32[3,1024]{1,0:T(4,128)S(1)}, f32[3,1024,1024]{2,1,0:T(8,128)}) fusion(bf16[1024,3,128]{2,0,1:T(8,128)(2,1)} %get-tuple-element.184, bf16[16,1024,3,128]{3,1,0,2:T(8,128)(2,1)} %get-tuple-element.183, s32[]{:T(128)} %get-tuple-element.170), kind=kOutput, calls=%fused_computation.1.clone.1 | convolution fusion | flops 811594752 | bytes 14168576 | tf_op jit(solution)/shard_map/while/body/eval_jaxpr/qhd,khd->hqk/dot_general | solution.py:20
  408.0 7.8 %bitcast_reduce_fusion.2 = (f32[3,1024]{1,0:T(4,128)S(1)}, f32[3,1024,1024]{2,1,0:T(8,128)}) fusion(bf16[1024,3,128]{2,0,1:T(8,128)(2,1)} %get-tuple-element.184, bf16[16,1024,3,128]{3,1,0,2:T(8,128)(2,1)} %get-tuple-element.183, s32[]{:T(128)} %get-tuple-element.170), kind=kOutput, calls=%fused_computation.1.clone.1 | convolution fusion | flops 811594752 | bytes 14168576 | tf_op jit(solution)/shard_map/while/body/eval_jaxpr/qhd,khd->hqk/dot_general | solution.py:20
  429.3 7.8 %bitcast_reduce_fusion.2 = (f32[3,1024]{1,0:T(4,128)S(1)}, f32[3,1024,1024]{2,1,0:T(8,128)}) fusion(bf16[1024,3,128]{2,0,1:T(8,128)(2,1)} %get-tuple-element.184, bf16[16,1024,3,128]{3,1,0,2:T(8,128)(2,1)} %get-tuple-element.183, s32[]{:T(128)} %get-tuple-element.170), kind=kOutput, calls=%fused_computation.1.clone.1 | convolution fusion | flops 811594752 | bytes 14168576 | tf_op jit(solution)/shard_map/while/body/eval_jaxpr/qhd,khd->hqk/dot_general | solution.py:20
  450.6 7.8 %bitcast_reduce_fusion.2 = (f32[3,1024]{1,0:T(4,128)S(1)}, f32[3,1024,1024]{2,1,0:T(8,128)}) fusion(bf16[1024,3,128]{2,0,1:T(8,128)(2,1)} %get-tuple-element.184, bf16[16,1024,3,128]{3,1,0,2:T(8,128)(2,1)} %get-tuple-element.183, s32[]{:T(128)} %get-tuple-element.170), kind=kOutput, calls=%fused_computation.1.clone.1 | convolution fusion | flops 811594752 | bytes 14168576 | tf_op jit(solution)/shard_map/while/body/eval_jaxpr/qhd,khd->hqk/dot_general | solution.py:20
  471.9 7.8 %bitcast_reduce_fusion.2 = (f32[3,1024]{1,0:T(4,128)S(1)}, f32[3,1024,1024]{2,1,0:T(8,128)}) fusion(bf16[1024,3,128]{2,0,1:T(8,128)(2,1)} %get-tuple-element.184, bf16[16,1024,3,128]{3,1,0,2:T(8,128)(2,1)} %get-tuple-element.183, s32[]{:T(128)} %get-tuple-element.170), kind=kOutput, calls=%fused_computation.1.clone.1 | convolution fusion | flops 811594752 | bytes 14168576 | tf_op jit(solution)/shard_map/while/body/eval_jaxpr/qhd,khd->hqk/dot_general | solution.py:20
  493.2 7.8 %bitcast_reduce_fusion.2 = (f32[3,1024]{1,0:T(4,128)S(1)}, f32[3,1024,1024]{2,1,0:T(8,128)}) fusion(bf16[1024,3,128]{2,0,1:T(8,128)(2,1)} %get-tuple-element.184, bf16[16,1024,3,128]{3,1,0,2:T(8,128)(2,1)} %get-tuple-element.183, s32[]{:T(128)} %get-tuple-element.170), kind=kOutput, calls=%fused_computation.1.clone.1 | convolution fusion | flops 811594752 | bytes 14168576 | tf_op jit(solution)/shard_map/while/body/eval_jaxpr/qhd,khd->hqk/dot_general | solution.py:20
  514.5 7.8 %bitcast_reduce_fusion.2 = (f32[3,1024]{1,0:T(4,128)S(1)}, f32[3,1024,1024]{2,1,0:T(8,128)}) fusion(bf16[1024,3,128]{2,0,1:T(8,128)(2,1)} %get-tuple-element.184, bf16[16,1024,3,128]{3,1,0,2:T(8,128)(2,1)} %get-tuple-element.183, s32[]{:T(128)} %get-tuple-element.170), kind=kOutput, calls=%fused_computation.1.clone.1 | convolution fusion | flops 811594752 | bytes 14168576 | tf_op jit(solution)/shard_map/while/body/eval_jaxpr/qhd,khd->hqk/dot_general | solution.py:20
  535.8 7.8 %bitcast_reduce_fusion.2 = (f32[3,1024]{1,0:T(4,128)S(1)}, f32[3,1024,1024]{2,1,0:T(8,128)}) fusion(bf16[1024,3,128]{2,0,1:T(8,128)(2,1)} %get-tuple-element.184, bf16[16,1024,3,128]{3,1,0,2:T(8,128)(2,1)} %get-tuple-element.183, s32[]{:T(128)} %get-tuple-element.170), kind=kOutput, calls=%fused_computation.1.clone.1 | convolution fusion | flops 811594752 | bytes 14168576 | tf_op jit(solution)/shard_map/while/body/eval_jaxpr/qhd,khd->hqk/dot_general | solution.py:20
  543.6 6.8 %fusion.37 = f32[3,1024]{1,0:T(4,128)S(1)} fusion(f32[3,1024,1024]{2,1,0:T(8,128)} %get-tuple-element.158, f32[3,1024]{1,0:T(4,128)S(1)} %select_maximum_fusion.2), kind=kLoop, calls=%fused_computation.4.clone.1 | loop fusion | flops 9434112 | bytes 12607488 | tf_op jit(solution)/shard_map/while/body/eval_jaxpr/reduce_sum | solution.py:25
  557.2 7.8 %bitcast_reduce_fusion.2 = (f32[3,1024]{1,0:T(4,128)S(1)}, f32[3,1024,1024]{2,1,0:T(8,128)}) fusion(bf16[1024,3,128]{2,0,1:T(8,128)(2,1)} %get-tuple-element.184, bf16[16,1024,3,128]{3,1,0,2:T(8,128)(2,1)} %get-tuple-element.183, s32[]{:T(128)} %get-tuple-element.170), kind=kOutput, calls=%fused_computation.1.clone.1 | convolution fusion | flops 811594752 | bytes 14168576 | tf_op jit(solution)/shard_map/while/body/eval_jaxpr/qhd,khd->hqk/dot_general | solution.py:20
  580.9 22.1 %all_to_all.64 = bf16[8,128,384]{1,2,0:T(8,128)(2,1)S(1)} all-to-all(bf16[8,128,384]{1,2,0:T(8,128)(2,1)S(1)} %copy.42), channel_id=1, replica_groups=mesh['blk'=16,'head'=8] {'head'}, dimensions={0} | all-to-all | bytes 1572864 | tf_op jit(solution)/shard_map/all_to_all | solution.py:74
  (141 shorter events, 199.7 us)
Async XLA Ops:
  9.3 9.0 %copy-start.2 = (bf16[128,3072]{1,0:T(8,128)(2,1)S(1)}, bf16[128,3072]{1,0:T(8,128)(2,1)}, u32[]{:S(2)}) copy-start(bf16[128,3072]{1,0:T(8,128)(2,1)} %param.9) | copy-start | bytes 2359300
  10.5 21.2 %all-to-all-start = ((bf16[128,8,384]{0,2,1:T(8,128)(2,1)}), bf16[128,8,384]{0,2,1:T(8,128)(2,1)S(1)}, u32[]{:S(2)}, u32[]{:S(2)}) async-start(bf16[128,8,384]{0,2,1:T(8,128)(2,1)} %bitcast), calls=%async_computation | async-start | bytes 1572864 | tf_op jit(solution)/shard_map/all_to_all | solution.py:44
  31.7 17.3 %all-to-all-start.1 = ((bf16[128,8,384]{0,2,1:T(8,128)(2,1)}), bf16[128,8,384]{0,2,1:T(8,128)(2,1)S(1)}, u32[]{:S(2)}, u32[]{:S(2)}) async-start(bf16[128,8,384]{0,2,1:T(8,128)(2,1)} %bitcast.2), calls=%async_computation.1 | async-start | bytes 1572864 | tf_op jit(solution)/shard_map/all_to_all | solution.py:45
  35.5 151.9 %all-gather.2.cloned.1.call-start = ((), (), s32[]{:S(2)}) async-start(), calls=%async_computation.4 | async-start | bytes 26738688 | tf_op jit(solution)/shard_map/all_gather | solution.py:57
  51.3 1.1 copy-start.1
  51.3 1.4 copy-start.3
  54.1 24.8 %all-to-all-start.2 = ((bf16[128,8,384]{0,2,1:T(8,128)(2,1)}), bf16[128,8,384]{0,2,1:T(8,128)(2,1)S(1)}, u32[]{:S(2)}, u32[]{:S(2)}) async-start(bf16[128,8,384]{0,2,1:T(8,128)(2,1)} %bitcast.5), calls=%async_computation.2 | async-start | bytes 1572864 | tf_op jit(solution)/shard_map/all_to_all | solution.py:43
  245.5 8.2 %copy-start = (f32[3,1024,1024]{2,1,0:T(8,128)S(1)}, f32[3,1024,1024]{2,1,0:T(8,128)}, u32[]{:S(2)}) copy-start(f32[3,1024,1024]{2,1,0:T(8,128)} %get-tuple-element.158) | copy-start | bytes 37748740 | tf_op jit(solution)/shard_map/while
  266.5 8.2 %copy-start = (f32[3,1024,1024]{2,1,0:T(8,128)S(1)}, f32[3,1024,1024]{2,1,0:T(8,128)}, u32[]{:S(2)}) copy-start(f32[3,1024,1024]{2,1,0:T(8,128)} %get-tuple-element.158) | copy-start | bytes 37748740 | tf_op jit(solution)/shard_map/while
  287.8 8.2 %copy-start = (f32[3,1024,1024]{2,1,0:T(8,128)S(1)}, f32[3,1024,1024]{2,1,0:T(8,128)}, u32[]{:S(2)}) copy-start(f32[3,1024,1024]{2,1,0:T(8,128)} %get-tuple-element.158) | copy-start | bytes 37748740 | tf_op jit(solution)/shard_map/while
  309.2 8.2 %copy-start = (f32[3,1024,1024]{2,1,0:T(8,128)S(1)}, f32[3,1024,1024]{2,1,0:T(8,128)}, u32[]{:S(2)}) copy-start(f32[3,1024,1024]{2,1,0:T(8,128)} %get-tuple-element.158) | copy-start | bytes 37748740 | tf_op jit(solution)/shard_map/while
  330.5 8.2 %copy-start = (f32[3,1024,1024]{2,1,0:T(8,128)S(1)}, f32[3,1024,1024]{2,1,0:T(8,128)}, u32[]{:S(2)}) copy-start(f32[3,1024,1024]{2,1,0:T(8,128)} %get-tuple-element.158) | copy-start | bytes 37748740 | tf_op jit(solution)/shard_map/while
  351.8 8.2 %copy-start = (f32[3,1024,1024]{2,1,0:T(8,128)S(1)}, f32[3,1024,1024]{2,1,0:T(8,128)}, u32[]{:S(2)}) copy-start(f32[3,1024,1024]{2,1,0:T(8,128)} %get-tuple-element.158) | copy-start | bytes 37748740 | tf_op jit(solution)/shard_map/while
  373.1 8.2 %copy-start = (f32[3,1024,1024]{2,1,0:T(8,128)S(1)}, f32[3,1024,1024]{2,1,0:T(8,128)}, u32[]{:S(2)}) copy-start(f32[3,1024,1024]{2,1,0:T(8,128)} %get-tuple-element.158) | copy-start | bytes 37748740 | tf_op jit(solution)/shard_map/while
  394.4 8.2 %copy-start = (f32[3,1024,1024]{2,1,0:T(8,128)S(1)}, f32[3,1024,1024]{2,1,0:T(8,128)}, u32[]{:S(2)}) copy-start(f32[3,1024,1024]{2,1,0:T(8,128)} %get-tuple-element.158) | copy-start | bytes 37748740 | tf_op jit(solution)/shard_map/while
  415.7 8.2 %copy-start = (f32[3,1024,1024]{2,1,0:T(8,128)S(1)}, f32[3,1024,1024]{2,1,0:T(8,128)}, u32[]{:S(2)}) copy-start(f32[3,1024,1024]{2,1,0:T(8,128)} %get-tuple-element.158) | copy-start | bytes 37748740 | tf_op jit(solution)/shard_map/while
  437.0 8.2 %copy-start = (f32[3,1024,1024]{2,1,0:T(8,128)S(1)}, f32[3,1024,1024]{2,1,0:T(8,128)}, u32[]{:S(2)}) copy-start(f32[3,1024,1024]{2,1,0:T(8,128)} %get-tuple-element.158) | copy-start | bytes 37748740 | tf_op jit(solution)/shard_map/while
  458.4 8.2 %copy-start = (f32[3,1024,1024]{2,1,0:T(8,128)S(1)}, f32[3,1024,1024]{2,1,0:T(8,128)}, u32[]{:S(2)}) copy-start(f32[3,1024,1024]{2,1,0:T(8,128)} %get-tuple-element.158) | copy-start | bytes 37748740 | tf_op jit(solution)/shard_map/while
  479.7 8.2 %copy-start = (f32[3,1024,1024]{2,1,0:T(8,128)S(1)}, f32[3,1024,1024]{2,1,0:T(8,128)}, u32[]{:S(2)}) copy-start(f32[3,1024,1024]{2,1,0:T(8,128)} %get-tuple-element.158) | copy-start | bytes 37748740 | tf_op jit(solution)/shard_map/while
  501.0 8.2 %copy-start = (f32[3,1024,1024]{2,1,0:T(8,128)S(1)}, f32[3,1024,1024]{2,1,0:T(8,128)}, u32[]{:S(2)}) copy-start(f32[3,1024,1024]{2,1,0:T(8,128)} %get-tuple-element.158) | copy-start | bytes 37748740 | tf_op jit(solution)/shard_map/while
  522.3 8.2 %copy-start = (f32[3,1024,1024]{2,1,0:T(8,128)S(1)}, f32[3,1024,1024]{2,1,0:T(8,128)}, u32[]{:S(2)}) copy-start(f32[3,1024,1024]{2,1,0:T(8,128)} %get-tuple-element.158) | copy-start | bytes 37748740 | tf_op jit(solution)/shard_map/while
  543.6 8.2 %copy-start = (f32[3,1024,1024]{2,1,0:T(8,128)S(1)}, f32[3,1024,1024]{2,1,0:T(8,128)}, u32[]{:S(2)}) copy-start(f32[3,1024,1024]{2,1,0:T(8,128)} %get-tuple-element.158) | copy-start | bytes 37748740 | tf_op jit(solution)/shard_map/while
  564.9 8.2 %copy-start = (f32[3,1024,1024]{2,1,0:T(8,128)S(1)}, f32[3,1024,1024]{2,1,0:T(8,128)}, u32[]{:S(2)}) copy-start(f32[3,1024,1024]{2,1,0:T(8,128)} %get-tuple-element.158) | copy-start | bytes 37748740 | tf_op jit(solution)/shard_map/while
Sparse Core Ops, SparseCore 0:
  51.4 135.9 all-gather.1
